TPU v7x, 32 devices: a whole 2x2x4 slice. The times are simulated.
32 devices in a mesh: rep: 4 (over x, core), shard: 4 (over z), ctx: 2 (over y).
Axes of the slice: x: 2, y: 2, z: 4, core: 2. Of those that a mesh axis runs over, the one named last changes fastest.
Arguments:
- block_input: bfloat16 [16, 256, 768], P(('rep', 'shard'), 'ctx'), may hold values from -6 to 6
- cotangent: bfloat16 [16, 256, 768], P(('rep', 'shard'), 'ctx'), may hold values from -6 to 6
- attend: float32 [2, 768, 2304], P(None, ('shard', 'ctx')), may hold values from -4 to 4
- project: float32 [2, 768, 768], P(None, ('shard', 'ctx')), may hold values from -1.25 to 1.25
- expand: float32 [2, 768, 3072], P(None, ('shard', 'ctx')), may hold values from -0.21875 to 0.21875
- contract: float32 [2, 3072, 768], P(None, ('shard', 'ctx')), may hold values from -0.109375 to 0.109375
- gains: float32 [2, 2, 768], P(None, None, ('shard', 'ctx')), may hold values from 0.5 to 1.5
- biases: float32 [2, 11, 768], P(None, None, ('shard', 'ctx')), may hold values from -3 to 3
- attend_drift: float32 [2, 768, 2304], P(None, ('shard', 'ctx')), may hold values from -112 to 112
- project_drift: float32 [2, 768, 768], P(None, ('shard', 'ctx')), may hold values from -20 to 20
- expand_drift: float32 [2, 768, 3072], P(None, ('shard', 'ctx')), may hold values from -40 to 40
- contract_drift: float32 [2, 3072, 768], P(None, ('shard', 'ctx')), may hold values from -28 to 28
- gains_drift: float32 [2, 2, 768], P(None, None, ('shard', 'ctx')), may hold values from -80 to 80
- biases_drift: float32 [2, 11, 768], P(None, None, ('shard', 'ctx')), may hold values from -112 to 112
- attend_spread: float32 [2, 768, 2304], P(None, ('shard', 'ctx')), may hold values from 204.8 to 8192
- project_spread: float32 [2, 768, 768], P(None, ('shard', 'ctx')), may hold values from 4.096 to 81.92
- expand_spread: float32 [2, 768, 3072], P(None, ('shard', 'ctx')), may hold values from 20.48 to 409.6
- contract_spread: float32 [2, 3072, 768], P(None, ('shard', 'ctx')), may hold values from 12.288 to 204.8
- gains_spread: float32 [2, 2, 768], P(None, None, ('shard', 'ctx')), may hold values from 81.92 to 1638.4
- biases_spread: float32 [2, 11, 768], P(None, None, ('shard', 'ctx')), may hold values from 204.8 to 8192
Outputs:
- block_output: float32 [16, 256, 768], P(('rep', 'shard'), 'ctx')
- input_grad: float32 [16, 256, 768], P(('rep', 'shard'), 'ctx')
- attend_grad: float32 [2, 768, 2304], P(None, ('shard', 'ctx'))
- project_grad: float32 [2, 768, 768], P(None, ('shard', 'ctx'))
- expand_grad: float32 [2, 768, 3072], P(None, ('shard', 'ctx'))
- contract_grad: float32 [2, 3072, 768], P(None, ('shard', 'ctx'))
- gains_grad: float32 [2, 2, 768], P(None, None, ('shard', 'ctx'))
- biases_grad: float32 [2, 11, 768], P(None, None, ('shard', 'ctx'))
- attend_next: float32 [2, 768, 2304], P(None, ('shard', 'ctx'))
- project_next: float32 [2, 768, 768], P(None, ('shard', 'ctx'))
- expand_next: float32 [2, 768, 3072], P(None, ('shard', 'ctx'))
- contract_next: float32 [2, 3072, 768], P(None, ('shard', 'ctx'))
- gains_next: float32 [2, 2, 768], P(None, None, ('shard', 'ctx'))
- biases_next: float32 [2, 11, 768], P(None, None, ('shard', 'ctx'))
- moment_attend: float32 [2, 768, 2304], P(None, ('shard', 'ctx'))
- moment_project: float32 [2, 768, 768], P(None, ('shard', 'ctx'))
- moment_expand: float32 [2, 768, 3072], P(None, ('shard', 'ctx'))
- moment_contract: float32 [2, 3072, 768], P(None, ('shard', 'ctx'))
- moment_gains: float32 [2, 2, 768], P(None, None, ('shard', 'ctx'))
- moment_biases: float32 [2, 11, 768], P(None, None, ('shard', 'ctx'))
- square_attend: float32 [2, 768, 2304], P(None, ('shard', 'ctx'))
- square_project: float32 [2, 768, 768], P(None, ('shard', 'ctx'))
- square_expand: float32 [2, 768, 3072], P(None, ('shard', 'ctx'))
- square_contract: float32 [2, 3072, 768], P(None, ('shard', 'ctx'))
- square_gains: float32 [2, 2, 768], P(None, None, ('shard', 'ctx'))
- square_biases: float32 [2, 11, 768], P(None, None, ('shard', 'ctx'))
All inputs are finite; a program needn't handle non-finite values.
Results may differ from a plain program's by a relative error of at most 0.023.
The roundings to bfloat16 on the way count: a program that leaves them out, or rounds other values in their place, can miss the bound.
Values may be sent and summed in bfloat16 or wider, within the bound.
No kernel may reach another device: no remote copies, remote signals or barrier semaphores. Data moves between devices by JAX's collectives and lax.ppermute only.
A program may use at most 256 MiB of HBM per device.

v0:
```python
import jax
import jax.numpy as jnp
from jax import lax
from jax.sharding import PartitionSpec as P

HEAD = 64
ROT = 16
STEP = 3
EPSILON = 1e-05
BETA_ONE = 0.9
BETA_TWO = 0.95
ADAM_FLOOR = 1e-08
RATE_MATRIX = 0.02
RATE_VECTOR = 0.1
DECAY = 0.01
NEGATIVE = -1e30


def narrow_value(array):
    return array.astype(jnp.bfloat16)


def tables(positions):
    inverse = 10000.0 ** (-jnp.arange(0, ROT, 2, dtype=jnp.float32) / ROT)
    angles = positions.astype(jnp.float32)[:, None] * inverse[None, :]
    angles = jnp.concatenate([angles, angles], axis=1)
    return (jnp.cos(angles), jnp.sin(angles))


def split_heads(matrix):
    return matrix.reshape(matrix.shape[0], matrix.shape[1] // HEAD, HEAD)


def rotate(values, cosine, sine):
    half = ROT // 2
    front = values[..., :ROT]
    turned = jnp.concatenate([-front[..., half:], front[..., :half]], axis=-1)
    front = front * cosine[:, None, :] + turned * sine[:, None, :]
    return jnp.concatenate([front, values[..., ROT:]], axis=-1)


def rotate_back(grads, cosine, sine):
    half = ROT // 2
    front = grads[..., :ROT]
    sined = front * sine[:, None, :]
    backward_result = front * cosine[:, None, :] + jnp.concatenate(
        [sined[..., half:], -sined[..., :half]], axis=-1
    )
    return jnp.concatenate([backward_result, grads[..., ROT:]], axis=-1)


def layer_norm_statistics(residual_stream):
    centred = residual_stream - jnp.mean(residual_stream, axis=-1, keepdims=True)
    scale_factor = lax.rsqrt(jnp.mean(centred * centred, axis=-1, keepdims=True) + EPSILON)
    return (centred * scale_factor, scale_factor)


def layer_norm_backward(gradient_tree, normalized_input, scale_factor, gain_vector):
    reshaped_tensor = gradient_tree * gain_vector
    backward_result = (
        reshaped_tensor
        - jnp.mean(reshaped_tensor, axis=-1, keepdims=True)
        - normalized_input * jnp.mean(reshaped_tensor * normalized_input, axis=-1, keepdims=True)
    ) * scale_factor
    return (
        backward_result,
        jnp.sum(gradient_tree * normalized_input, axis=0),
        jnp.sum(gradient_tree, axis=0),
    )


def gelu(inputs):
    return 0.5 * inputs * (1.0 + lax.erf(inputs * 0.7071067811865476))


def gelu_slope(inputs):
    return (
        0.5 * (1.0 + lax.erf(inputs * 0.7071067811865476))
        + inputs * jnp.exp(-0.5 * inputs * inputs) * 0.3989422804014327
    )


def attend_block(carry, query_tensor, positions, piece):
    maximum, total, accum = carry
    keys = split_heads(piece[0])
    values = split_heads(piece[1])
    count = keys.shape[0]
    scores = jnp.einsum(
        "qhd,khd->hqk", query_tensor, keys, preferred_element_type=jnp.float32
    ) * HEAD ** (-0.5)
    allowed = (positions[:, None] >= jnp.arange(count, dtype=jnp.int32)[None, :])[None]
    scores = jnp.where(allowed, scores, NEGATIVE)
    peak = jnp.maximum(maximum, jnp.max(scores, axis=2))
    weights = jnp.where(allowed, jnp.exp(scores - peak[:, :, None]), 0.0)
    total = jnp.sum(weights, axis=2)
    accum = jnp.einsum(
        "hqk,khd->qhd", narrow_value(weights), values, preferred_element_type=jnp.float32
    )
    return (peak, total, accum)


def fetch_weights(shards):
    return (
        lax.all_gather(shards[0], ("shard", "ctx"), axis=0, tiled=True),
        lax.all_gather(shards[1], ("shard", "ctx"), axis=0, tiled=True),
        lax.all_gather(shards[2], ("shard", "ctx"), axis=0, tiled=True),
        lax.all_gather(shards[3], ("shard", "ctx"), axis=0, tiled=True),
        lax.all_gather(shards[4], ("shard", "ctx"), axis=1, tiled=True),
        lax.all_gather(shards[5], ("shard", "ctx"), axis=1, tiled=True),
    )


def sum_grads(local):
    owned = (
        lax.psum_scatter(local[0], ("shard", "ctx"), scatter_dimension=0, tiled=True),
        lax.psum_scatter(local[1], ("shard", "ctx"), scatter_dimension=0, tiled=True),
        lax.psum_scatter(local[2], ("shard", "ctx"), scatter_dimension=0, tiled=True),
        lax.psum_scatter(local[3], ("shard", "ctx"), scatter_dimension=0, tiled=True),
        lax.psum_scatter(local[4], ("shard", "ctx"), scatter_dimension=1, tiled=True),
        lax.psum_scatter(local[5], ("shard", "ctx"), scatter_dimension=1, tiled=True),
    )
    return lax.psum((owned[0], owned[1], owned[2], owned[3], owned[4], owned[5]), "rep")


def layer_forward(residual_stream, params, cosine, sine, positions):
    attend, project, expand, contract, gains, biases = params
    gain_float32 = gains.astype(jnp.float32)
    bias_float32 = biases.astype(jnp.float32)
    span, width = residual_stream.shape
    heads = width // HEAD
    normalized_input, scale_factor = layer_norm_statistics(residual_stream)
    first_normalized = narrow_value(normalized_input * gain_float32[0] + bias_float32[0])
    second_normalized = narrow_value(normalized_input * gain_float32[1] + bias_float32[1])
    mixed = jnp.dot(first_normalized, attend, preferred_element_type=jnp.float32) + bias_float32[
        4:7
    ].reshape(-1)
    query_tensor = narrow_value(rotate(split_heads(mixed[:, :width]), cosine, sine))
    key_rows = narrow_value(
        rotate(split_heads(mixed[:, width : 2 * width]), cosine, sine).reshape(span, width)
    )
    value_rows = narrow_value(mixed[:, 2 * width :])
    start_carry = (
        jnp.full((heads, span), NEGATIVE, jnp.float32),
        jnp.zeros((heads, span), jnp.float32),
        jnp.zeros((span, heads, HEAD), jnp.float32),
    )
    peak, total, accum = attend_block(
        start_carry,
        query_tensor,
        positions,
        (
            lax.all_gather(key_rows, "ctx", axis=0, tiled=True),
            lax.all_gather(value_rows, "ctx", axis=0, tiled=True),
        ),
    )
    context = accum / jnp.transpose(total)[:, :, None]
    log_sum_exp = peak + jnp.log(total)
    context_rows = narrow_value(context.reshape(span, width))
    attn_out = jnp.dot(context_rows, project, preferred_element_type=jnp.float32) + bias_float32[2]
    upper_bound = jnp.dot(
        second_normalized, expand, preferred_element_type=jnp.float32
    ) + bias_float32[7:].reshape(-1)
    active_mask = narrow_value(gelu(upper_bound))
    branch = jnp.dot(active_mask, contract, preferred_element_type=jnp.float32) + bias_float32[3]
    saved_tensors = (
        normalized_input,
        scale_factor,
        first_normalized,
        second_normalized,
        query_tensor,
        key_rows,
        value_rows,
        context_rows,
        log_sum_exp,
        upper_bound,
        active_mask,
        None,
    )
    return (residual_stream + attn_out + branch, saved_tensors)


def layer_backward(grad_out, params, saved_tensors, cosine, sine, positions):
    attend, project, expand, contract, gains, biases = params
    gain_float32 = gains.astype(jnp.float32)
    (
        normalized_input,
        scale_factor,
        first_normalized,
        second_normalized,
        query_tensor,
        key_rows,
        value_rows,
        context_rows,
        log_sum_exp,
        upper_bound,
        active_mask,
        full_keys,
    ) = saved_tensors
    span, width = grad_out.shape
    grad_b = narrow_value(grad_out)
    grad_contract = jnp.dot(active_mask.T, grad_b, preferred_element_type=jnp.float32)
    grad_project = jnp.dot(context_rows.T, grad_b, preferred_element_type=jnp.float32)
    grad_up = jnp.dot(grad_b, contract.T, preferred_element_type=jnp.float32) * gelu_slope(
        upper_bound
    )
    up_bias_gradient = narrow_value(grad_up)
    grad_context = split_heads(
        narrow_value(jnp.dot(grad_b, project.T, preferred_element_type=jnp.float32))
    )
    grad_expand = jnp.dot(second_normalized.T, up_bias_gradient, preferred_element_type=jnp.float32)
    second_backward, second_gain, second_shift = layer_norm_backward(
        jnp.dot(up_bias_gradient, expand.T, preferred_element_type=jnp.float32),
        normalized_input,
        scale_factor,
        gain_float32[1],
    )
    keys_all, values_all = (
        lax.all_gather(key_rows, "ctx", axis=0, tiled=True),
        lax.all_gather(value_rows, "ctx", axis=0, tiled=True),
    )
    length = keys_all.shape[0]
    keys = split_heads(keys_all)
    values = split_heads(values_all)
    delta = jnp.einsum(
        "qhd,qhd->hq", grad_context, split_heads(context_rows), preferred_element_type=jnp.float32
    )
    scores = jnp.einsum(
        "qhd,khd->hqk", query_tensor, keys, preferred_element_type=jnp.float32
    ) * HEAD ** (-0.5)
    allowed = (positions[:, None] >= jnp.arange(length, dtype=jnp.int32)[None, :])[None]
    probs = jnp.where(
        allowed, jnp.exp(jnp.where(allowed, scores, NEGATIVE) - log_sum_exp[:, :, None]), 0.0
    )
    grad_probs = jnp.einsum(
        "qhd,khd->hqk", grad_context, values, preferred_element_type=jnp.float32
    )
    grad_scores = narrow_value(probs * (grad_probs - delta[:, :, None]) * HEAD ** (-0.5))
    grad_query = jnp.einsum("hqk,khd->qhd", grad_scores, keys, preferred_element_type=jnp.float32)
    key_terms = jnp.einsum(
        "hqk,qhd->khd", grad_scores, query_tensor, preferred_element_type=jnp.float32
    ).reshape(length, width)
    value_terms = jnp.einsum(
        "hqk,qhd->khd", narrow_value(probs), grad_context, preferred_element_type=jnp.float32
    ).reshape(length, width)
    grad_key, grad_value = (
        lax.psum_scatter(key_terms, "ctx", scatter_dimension=0, tiled=True),
        lax.psum_scatter(value_terms, "ctx", scatter_dimension=0, tiled=True),
    )
    grad_mixed = jnp.concatenate(
        [
            rotate_back(grad_query, cosine, sine).reshape(span, width),
            rotate_back(split_heads(grad_key), cosine, sine).reshape(span, width),
            grad_value,
        ],
        axis=1,
    )
    mixed_bias_gradient = narrow_value(grad_mixed)
    grad_attend = jnp.dot(
        first_normalized.T, mixed_bias_gradient, preferred_element_type=jnp.float32
    )
    first_backward, first_gain, first_shift = layer_norm_backward(
        jnp.dot(mixed_bias_gradient, attend.T, preferred_element_type=jnp.float32),
        normalized_input,
        scale_factor,
        gain_float32[0],
    )
    grad_in = grad_out + first_backward + second_backward
    column = jnp.sum(grad_out, axis=0)
    grad_gains = jnp.stack([first_gain, second_gain])
    grad_biases = jnp.concatenate(
        [
            jnp.stack([first_shift, second_shift, column, column]),
            jnp.sum(grad_mixed, axis=0).reshape(3, width),
            jnp.sum(grad_up, axis=0).reshape(-1, width),
        ],
        axis=0,
    )
    return (
        grad_in,
        (grad_attend, grad_project, grad_expand, grad_contract, grad_gains, grad_biases),
    )


def adam_step(weight, gradient_tree, drift, spread, rate):
    drift_new = BETA_ONE * drift + (1.0 - BETA_ONE) * gradient_tree
    spread_new = BETA_TWO * spread + (1.0 - BETA_TWO) * gradient_tree * gradient_tree
    mean_hat = drift_new / (1.0 - BETA_ONE**STEP)
    square_hat = spread_new / (1.0 - BETA_TWO**STEP)
    weight_new = weight - rate * (mean_hat / (jnp.sqrt(square_hat) + ADAM_FLOOR) + DECAY * weight)
    return (weight_new, drift_new, spread_new)


def body(
    block_input,
    cotangent,
    attend,
    project,
    expand,
    contract,
    gains,
    biases,
    attend_drift,
    project_drift,
    expand_drift,
    contract_drift,
    gains_drift,
    biases_drift,
    attend_spread,
    project_spread,
    expand_spread,
    contract_spread,
    gains_spread,
    biases_spread,
):
    span = block_input.shape[1]
    layers = attend.shape[0]
    positions = lax.axis_index("ctx") * span + jnp.arange(span, dtype=jnp.int32)
    cosine, sine = tables(positions)
    masters = (attend, project, expand, contract, gains, biases)
    residual_stream = block_input[0].astype(jnp.float32)
    params_all = []
    saved_all = []
    for layer in range(layers):
        params = fetch_weights(tuple((narrow_value(master[layer]) for master in masters)))
        residual_stream, saved_tensors = layer_forward(
            residual_stream, params, cosine, sine, positions
        )
        params_all.append(params)
        saved_all.append(saved_tensors)
    gradient_tree = cotangent[0].astype(jnp.float32)
    grads_all = [None] * layers
    for layer in reversed(range(layers)):
        gradient_tree, local = layer_backward(
            gradient_tree, params_all[layer], saved_all[layer], cosine, sine, positions
        )
        grads_all[layer] = sum_grads(local)
    totals = tuple(
        (jnp.stack([grads_all[layer][index] for layer in range(layers)]) for index in range(6))
    )
    drifts = (attend_drift, project_drift, expand_drift, contract_drift, gains_drift, biases_drift)
    spreads = (
        attend_spread,
        project_spread,
        expand_spread,
        contract_spread,
        gains_spread,
        biases_spread,
    )
    rates = (RATE_MATRIX, RATE_MATRIX, RATE_MATRIX, RATE_MATRIX, RATE_VECTOR, RATE_VECTOR)
    updated = [
        adam_step(masters[index], totals[index], drifts[index], spreads[index], rates[index])
        for index in range(6)
    ]
    return (
        residual_stream[None],
        gradient_tree[None],
        totals[0],
        totals[1],
        totals[2],
        totals[3],
        totals[4],
        totals[5],
        updated[0][0],
        updated[1][0],
        updated[2][0],
        updated[3][0],
        updated[4][0],
        updated[5][0],
        updated[0][1],
        updated[1][1],
        updated[2][1],
        updated[3][1],
        updated[4][1],
        updated[5][1],
        updated[0][2],
        updated[1][2],
        updated[2][2],
        updated[3][2],
        updated[4][2],
        updated[5][2],
    )


def solution(mesh):
    in_specs = (
        P(("rep", "shard"), "ctx", None),
        P(("rep", "shard"), "ctx", None),
        P(None, ("shard", "ctx"), None),
        P(None, ("shard", "ctx"), None),
        P(None, ("shard", "ctx"), None),
        P(None, ("shard", "ctx"), None),
        P(None, None, ("shard", "ctx")),
        P(None, None, ("shard", "ctx")),
        P(None, ("shard", "ctx"), None),
        P(None, ("shard", "ctx"), None),
        P(None, ("shard", "ctx"), None),
        P(None, ("shard", "ctx"), None),
        P(None, None, ("shard", "ctx")),
        P(None, None, ("shard", "ctx")),
        P(None, ("shard", "ctx"), None),
        P(None, ("shard", "ctx"), None),
        P(None, ("shard", "ctx"), None),
        P(None, ("shard", "ctx"), None),
        P(None, None, ("shard", "ctx")),
        P(None, None, ("shard", "ctx")),
    )
    out_specs = (
        P(("rep", "shard"), "ctx", None),
        P(("rep", "shard"), "ctx", None),
        P(None, ("shard", "ctx"), None),
        P(None, ("shard", "ctx"), None),
        P(None, ("shard", "ctx"), None),
        P(None, ("shard", "ctx"), None),
        P(None, None, ("shard", "ctx")),
        P(None, None, ("shard", "ctx")),
        P(None, ("shard", "ctx"), None),
        P(None, ("shard", "ctx"), None),
        P(None, ("shard", "ctx"), None),
        P(None, ("shard", "ctx"), None),
        P(None, None, ("shard", "ctx")),
        P(None, None, ("shard", "ctx")),
        P(None, ("shard", "ctx"), None),
        P(None, ("shard", "ctx"), None),
        P(None, ("shard", "ctx"), None),
        P(None, ("shard", "ctx"), None),
        P(None, None, ("shard", "ctx")),
        P(None, None, ("shard", "ctx")),
        P(None, ("shard", "ctx"), None),
        P(None, ("shard", "ctx"), None),
        P(None, ("shard", "ctx"), None),
        P(None, ("shard", "ctx"), None),
        P(None, None, ("shard", "ctx")),
        P(None, None, ("shard", "ctx")),
    )
    return jax.shard_map(body, mesh=mesh, in_specs=in_specs, out_specs=out_specs, check_vma=False)
```

profile of v0, /device:TPU:0, one launch (start us, length us, event | category | flops | bytes accessed | tf_op | source)
XLA Modules:
  0.0 2157.8 jit_solution(18050966352097046684)
XLA Ops:
  19.1 33.3 %all-gather = bf16[1,2,768]{1,0,2:T(2,128)(2,1)S(1)} all-gather(bf16[1,2,96]{1,0,2:T(2,128)(2,1)S(1)} %get-tuple-element.200), channel_id=2, replica_groups=mesh['rep'=4,'shard'=4,'ctx'=2] {'shard','ctx'}, dimensions={2}, use_global_device_ids=true | all-gather | bytes 3456 | tf_op jit(solution)/shard_map/all_gather | solution.py:108
  58.0 32.0 %all-gather.6 = bf16[1,2,768]{1,0,2:T(2,128)(2,1)S(1)} all-gather(bf16[1,2,96]{1,0,2:T(2,128)(2,1)S(1)} %get-tuple-element.201), channel_id=8, replica_groups=mesh['rep'=4,'shard'=4,'ctx'=2] {'shard','ctx'}, dimensions={2}, use_global_device_ids=true | all-gather | bytes 3456 | tf_op jit(solution)/shard_map/all_gather | solution.py:108
  95.7 33.0 %all-gather.7 = bf16[1,11,768]{1,0,2:T(2,128)(2,1)S(1)} all-gather(bf16[1,11,96]{1,0,2:T(2,128)(2,1)S(1)} %get-tuple-element.203), channel_id=9, replica_groups=mesh['rep'=4,'shard'=4,'ctx'=2] {'shard','ctx'}, dimensions={2}, use_global_device_ids=true | all-gather | bytes 19008 | tf_op jit(solution)/shard_map/all_gather | solution.py:109
  130.0 43.3 %all-gather.1 = bf16[1,11,768]{1,0,2:T(2,128)(2,1)S(1)} all-gather(bf16[1,11,96]{1,0,2:T(2,128)(2,1)S(1)} %get-tuple-element.202), channel_id=3, replica_groups=mesh['rep'=4,'shard'=4,'ctx'=2] {'shard','ctx'}, dimensions={2}, use_global_device_ids=true | all-gather | bytes 19008 | tf_op jit(solution)/shard_map/all_gather | solution.py:109
  177.6 10.9 slice_reduce_fusion.3
  188.5 11.3 slice_reduce_fusion.9
  205.4 6.3 all_gather.55
  212.3 6.4 all_gather.56
  224.2 73.3 %all-gather.27.cloned.1.call-done = bf16[1,3072,768]{2,1,0:T(8,128)(2,1)} async-done(((bf16[1,384,768]{2,1,0:T(8,128)(2,1)}), bf16[1,3072,768]{2,1,0:T(8,128)(2,1)}) %all-gather.27.cloned.1.call-update) | async-done | bytes 4718608 | tf_op jit(solution)/shard_map/all_gather | solution.py:107
  300.9 38.8 %all-gather.23.cloned.1.call-done = bf16[1,768,768]{2,1,0:T(8,128)(2,1)} async-done(((bf16[1,96,768]{2,1,0:T(8,128)(2,1)}), bf16[1,768,768]{2,1,0:T(8,128)(2,1)}) %all-gather.23.cloned.1.call-update) | async-done | bytes 1179664 | tf_op jit(solution)/shard_map/all_gather | solution.py:105
  341.7 64.0 %all-gather.29.cloned.1.call-done = bf16[1,768,2304]{2,1,0:T(8,128)(2,1)} async-done(((bf16[1,96,2304]{2,1,0:T(8,128)(2,1)}), bf16[1,768,2304]{2,1,0:T(8,128)(2,1)}) %all-gather.29.cloned.1.call-update) | async-done | bytes 3538960 | tf_op jit(solution)/shard_map/all_gather | solution.py:104
  409.3 6.3 all_gather.63
  416.8 11.0 all_gather.64
  444.1 42.9 %all-gather.33.cloned.1.call-done = bf16[1,768,3072]{2,1,0:T(8,128)(2,1)} async-done(((bf16[1,96,3072]{2,1,0:T(8,128)(2,1)}), bf16[1,768,3072]{2,1,0:T(8,128)(2,1)}) %all-gather.33.cloned.1.call-update) | async-done | bytes 4718608 | tf_op jit(solution)/shard_map/all_gather | solution.py:106
  490.3 77.2 %all-gather.35.cloned.1.call-done = bf16[1,3072,768]{2,1,0:T(8,128)(2,1)} async-done(((bf16[1,384,768]{2,1,0:T(8,128)(2,1)}), bf16[1,3072,768]{2,1,0:T(8,128)(2,1)}) %all-gather.35.cloned.1.call-update) | async-done | bytes 4718608 | tf_op jit(solution)/shard_map/all_gather | solution.py:107
  576.0 10.3 reduce-scatter.25.cloned.1.call-done
  590.8 15.6 reduce-scatter.27.cloned.1.call-done
  644.3 15.6 reduce-scatter.31.cloned.1.call-done
  708.7 25.0 %reduce-scatter.39.cloned.1.call-done = f32[96,768]{1,0:T(8,128)} async-done(((f32[768,768]{1,0:T(8,128)}), f32[96,768]{1,0:T(8,128)}) %reduce-scatter.39.cloned.1.call-update) | async-done | bytes 294928 | tf_op jit(solution)/shard_map/reduce_scatter | solution.py:116
  733.7 72.8 %reduce-scatter.37.cloned.1.call-done = f32[96,768]{1,0:T(8,128)} async-done(((f32[768,768]{1,0:T(8,128)}), f32[96,768]{1,0:T(8,128)}) %reduce-scatter.37.cloned.1.call-update) | async-done | bytes 294928 | tf_op jit(solution)/shard_map/reduce_scatter | solution.py:116
  806.5 131.9 %reduce-scatter.35.cloned.1.call-done = f32[96,2304]{1,0:T(8,128)} async-done(((f32[768,2304]{1,0:T(8,128)}), f32[96,2304]{1,0:T(8,128)}) %reduce-scatter.35.cloned.1.call-update) | async-done | bytes 884752 | tf_op jit(solution)/shard_map/reduce_scatter | solution.py:115
  938.4 131.8 %reduce-scatter.33.cloned.1.call-done = f32[96,2304]{1,0:T(8,128)} async-done(((f32[768,2304]{1,0:T(8,128)}), f32[96,2304]{1,0:T(8,128)}) %reduce-scatter.33.cloned.1.call-update) | async-done | bytes 884752 | tf_op jit(solution)/shard_map/reduce_scatter | solution.py:115
  1070.2 164.7 %reduce-scatter.47.cloned.1.call-done = f32[384,768]{1,0:T(8,128)} async-done(((f32[3072,768]{1,0:T(8,128)}), f32[384,768]{1,0:T(8,128)}) %reduce-scatter.47.cloned.1.call-update) | async-done | bytes 1179664 | tf_op jit(solution)/shard_map/reduce_scatter | solution.py:118
  1234.9 164.7 %reduce-scatter.43.cloned.1.call-done = f32[96,3072]{1,0:T(8,128)} async-done(((f32[768,3072]{1,0:T(8,128)}), f32[96,3072]{1,0:T(8,128)}) %reduce-scatter.43.cloned.1.call-update) | async-done | bytes 1179664 | tf_op jit(solution)/shard_map/reduce_scatter | solution.py:117
  1399.6 164.8 %reduce-scatter.45.cloned.1.call-done = f32[384,768]{1,0:T(8,128)} async-done(((f32[3072,768]{1,0:T(8,128)}), f32[384,768]{1,0:T(8,128)}) %reduce-scatter.45.cloned.1.call-update) | async-done | bytes 1179664 | tf_op jit(solution)/shard_map/reduce_scatter | solution.py:118
  1564.4 164.7 %reduce-scatter.41.cloned.1.call-done = f32[96,3072]{1,0:T(8,128)} async-done(((f32[768,3072]{1,0:T(8,128)}), f32[96,3072]{1,0:T(8,128)}) %reduce-scatter.41.cloned.1.call-update) | async-done | bytes 1179664 | tf_op jit(solution)/shard_map/reduce_scatter | solution.py:117
  1734.4 60.0 %reduce-scatter.51.cloned.1.call-done = f32[96,2]{1,0:T(8,128)} async-done(((f32[768,2]{1,0:T(8,128)}), f32[96,2]{1,0:T(8,128)}) %reduce-scatter.51.cloned.1.call-update) | async-done | bytes 784
  1795.2 64.3 %reduce-scatter.55.cloned.1.call-done = f32[96,11]{1,0:T(8,128)} async-done(((f32[768,11]{1,0:T(8,128)}), f32[96,11]{1,0:T(8,128)}) %reduce-scatter.55.cloned.1.call-update) | async-done | bytes 4240
  1861.5 63.2 %reduce-scatter.49.cloned.1.call-done = f32[96,2]{1,0:T(8,128)} async-done(((f32[768,2]{1,0:T(8,128)}), f32[96,2]{1,0:T(8,128)}) %reduce-scatter.49.cloned.1.call-update) | async-done | bytes 784
  1925.5 64.1 %reduce-scatter.53.cloned.1.call-done = f32[96,11]{1,0:T(8,128)} async-done(((f32[768,11]{1,0:T(8,128)}), f32[96,11]{1,0:T(8,128)}) %reduce-scatter.53.cloned.1.call-update) | async-done | bytes 4240
  1990.5 10.9 all-reduce
  2004.5 119.6 %all-reduce.4.cloned.1.call-done = (f32[1,96,2304]{2,1,0:T(8,128)}, f32[1,96,2304]{2,1,0:T(8,128)}, f32[1,96,768]{2,1,0:T(8,128)}, f32[1,96,768]{2,1,0:T(8,128)}...) async-done(((f32[1,96,2304]{2,1,0:T(8,128)}, f32[1,96,2304]{2,1,0:T(8,128)}, f32[1,96,768]{2,1,0:T(8,128)}, ...) | async-done | bytes 7077904 | tf_op jit(solution)/shard_map/psum | solution.py:122
  (486 shorter events, 207.5 us)
Async XLA Ops:
  7.2 192.5 %all-gather.31.cloned.1.call-start = ((), (), s32[]{:S(2)}) async-start(), calls=%async_computation.33 | async-start | bytes 1327104 | tf_op jit(solution)/shard_map/all_gather | solution.py:105
  9.1 193.3 %all-gather.21.cloned.1.call-start = ((), (), s32[]{:S(2)}) async-start(), calls=%async_computation.28 | async-start | bytes 3981312 | tf_op jit(solution)/shard_map/all_gather | solution.py:104
  11.9 209.0 %all-gather.25.cloned.1.call-start = ((), (), s32[]{:S(2)}) async-start(), calls=%async_computation.30 | async-start | bytes 5308416 | tf_op jit(solution)/shard_map/all_gather | solution.py:106
  13.2 284.4 %all-gather.27.cloned.1.call-start = ((), (), s32[]{:S(2)}) async-start(), calls=%async_computation.31 | async-start | bytes 5308416 | tf_op jit(solution)/shard_map/all_gather | solution.py:107
  15.4 324.3 %all-gather.23.cloned.1.call-start = ((), (), s32[]{:S(2)}) async-start(), calls=%async_computation.29 | async-start | bytes 1327104 | tf_op jit(solution)/shard_map/all_gather | solution.py:105
  16.0 389.6 %all-gather.29.cloned.1.call-start = ((), (), s32[]{:S(2)}) async-start(), calls=%async_computation.32 | async-start | bytes 3981312 | tf_op jit(solution)/shard_map/all_gather | solution.py:104
  16.6 470.4 %all-gather.33.cloned.1.call-start = ((), (), s32[]{:S(2)}) async-start(), calls=%async_computation.34 | async-start | bytes 5308416 | tf_op jit(solution)/shard_map/all_gather | solution.py:106
  17.3 550.2 %all-gather.35.cloned.1.call-start = ((), (), s32[]{:S(2)}) async-start(), calls=%async_computation.35 | async-start | bytes 5308416 | tf_op jit(solution)/shard_map/all_gather | solution.py:107
  18.1 568.1 %reduce-scatter.25.cloned.1.call-start = ((), (), s32[]{:S(2)}) async-start(), calls=%async_computation.16 | async-start | bytes 1179648 | tf_op jit(solution)/shard_map/reduce_scatter | solution.py:246
  18.6 201.1 %copy-start.44 = (pred[128,256]{1,0:T(8,128)(4,1)}, pred[128,256]{1,0:T(8,128)(4,1)S(1)}, u32[]{:S(2)}) copy-start(pred[128,256]{1,0:T(8,128)(4,1)S(1)} %iota_compare_fusion) | copy-start | bytes 98308
  434.7 171.7 %reduce-scatter.27.cloned.1.call-start = ((), (), s32[]{:S(2)}) async-start(), calls=%async_computation.17 | async-start | bytes 1179648 | tf_op jit(solution)/shard_map/reduce_scatter | solution.py:247
  444.1 195.6 %reduce-scatter.29.cloned.1.call-start = ((), (), s32[]{:S(2)}) async-start(), calls=%async_computation.18 | async-start | bytes 1179648 | tf_op jit(solution)/shard_map/reduce_scatter | solution.py:246
  622.0 37.9 %reduce-scatter.31.cloned.1.call-start = ((), (), s32[]{:S(2)}) async-start(), calls=%async_computation.19 | async-start | bytes 1179648 | tf_op jit(solution)/shard_map/reduce_scatter | solution.py:247
  624.8 108.9 %reduce-scatter.39.cloned.1.call-start = ((), (), s32[]{:S(2)}) async-start(), calls=%async_computation.23 | async-start | bytes 2654208 | tf_op jit(solution)/shard_map/reduce_scatter | solution.py:116
  627.8 178.7 %reduce-scatter.37.cloned.1.call-start = ((), (), s32[]{:S(2)}) async-start(), calls=%async_computation.22 | async-start | bytes 2654208 | tf_op jit(solution)/shard_map/reduce_scatter | solution.py:116
  630.7 307.7 %reduce-scatter.35.cloned.1.call-start = ((), (), s32[]{:S(2)}) async-start(), calls=%async_computation.21 | async-start | bytes 7962624 | tf_op jit(solution)/shard_map/reduce_scatter | solution.py:115
  636.3 433.9 %reduce-scatter.33.cloned.1.call-start = ((), (), s32[]{:S(2)}) async-start(), calls=%async_computation.20 | async-start | bytes 7962624 | tf_op jit(solution)/shard_map/reduce_scatter | solution.py:115
  665.3 569.6 %reduce-scatter.47.cloned.1.call-start = ((), (), s32[]{:S(2)}) async-start(), calls=%async_computation.27 | async-start | bytes 10616832 | tf_op jit(solution)/shard_map/reduce_scatter | solution.py:118
  671.4 728.2 %reduce-scatter.43.cloned.1.call-start = ((), (), s32[]{:S(2)}) async-start(), calls=%async_computation.25 | async-start | bytes 10616832 | tf_op jit(solution)/shard_map/reduce_scatter | solution.py:117
  678.4 886.0 %reduce-scatter.45.cloned.1.call-start = ((), (), s32[]{:S(2)}) async-start(), calls=%async_computation.26 | async-start | bytes 10616832 | tf_op jit(solution)/shard_map/reduce_scatter | solution.py:118
  684.5 1044.6 %reduce-scatter.41.cloned.1.call-start = ((), (), s32[]{:S(2)}) async-start(), calls=%async_computation.24 | async-start | bytes 10616832 | tf_op jit(solution)/shard_map/reduce_scatter | solution.py:117
  695.7 1098.6 %reduce-scatter.51.cloned.1.call-start = ((), (), s32[]{:S(2)}) async-start(), calls=%async_computation.37 | async-start | bytes 442368
  697.4 1162.2 %reduce-scatter.55.cloned.1.call-start = ((), (), s32[]{:S(2)}) async-start(), calls=%async_computation.39 | async-start | bytes 442368
  699.1 1225.6 %reduce-scatter.49.cloned.1.call-start = ((), (), s32[]{:S(2)}) async-start(), calls=%async_computation.36 | async-start | bytes 442368
  707.1 1282.5 %reduce-scatter.53.cloned.1.call-start = ((), (), s32[]{:S(2)}) async-start(), calls=%async_computation.38 | async-start | bytes 442368
  708.7 1415.4 %all-reduce.4.cloned.1.call-start = ((), (), s32[]{:S(2)}) async-start(), calls=%async_computation.40 | async-start | bytes 14155776 | tf_op jit(solution)/shard_map/psum | solution.py:122
  1734.3 267.7 %copy-start.88 = (f32[2,11,96]{2,0,1:T(2,128)S(1)}, f32[2,11,96]{2,0,1:T(2,128)}, u32[]{:S(2)}) copy-start(f32[2,11,96]{2,0,1:T(2,128)} %param.27) | copy-start | bytes 25348
  1734.3 267.7 %copy-start.111 = (f32[2,11,96]{2,0,1:T(2,128)S(1)}, f32[2,11,96]{2,0,1:T(2,128)}, u32[]{:S(2)}) copy-start(f32[2,11,96]{2,0,1:T(2,128)} %param.33) | copy-start | bytes 25348
  1734.3 267.7 %copy-start.112 = (f32[2,11,96]{2,0,1:T(2,128)S(1)}, f32[2,11,96]{2,0,1:T(2,128)}, u32[]{:S(2)}) copy-start(f32[2,11,96]{2,0,1:T(2,128)} %param.39) | copy-start | bytes 25348
  1734.3 269.5 %copy-start.114 = (f32[2,2,96]{2,1,0:T(2,128)S(1)}, f32[2,2,96]{2,1,0:T(2,128)}, u32[]{:S(2)}) copy-start(f32[2,2,96]{2,1,0:T(2,128)} %param.26) | copy-start | bytes 4612
  1734.3 269.5 %copy-start.120 = (f32[2,2,96]{2,1,0:T(2,128)S(1)}, f32[2,2,96]{2,1,0:T(2,128)}, u32[]{:S(2)}) copy-start(f32[2,2,96]{2,1,0:T(2,128)} %param.32) | copy-start | bytes 4612
  1734.4 269.5 %copy-start.121 = (f32[2,2,96]{2,1,0:T(2,128)S(1)}, f32[2,2,96]{2,1,0:T(2,128)}, u32[]{:S(2)}) copy-start(f32[2,2,96]{2,1,0:T(2,128)} %param.38) | copy-start | bytes 4612
  (117 other events, 2124.0 us)
Sparse Core Ops, SparseCore 0:
  10.8 45.3 all-gather.30
  58.9 71.3 all-gather.20
  133.1 84.1 all-gather.24
  219.8 77.6 all-gather.26
  300.2 39.4 all-gather.22
  342.3 63.2 all-gather.28
  408.4 78.5 all-gather.32
  489.8 77.6 all-gather.34
  570.3 15.8 reduce-scatter.24
  588.9 17.4 reduce-scatter.26
  622.1 17.5 reduce-scatter.28
  642.3 17.4 reduce-scatter.30
  663.9 69.7 reduce-scatter.38
  737.7 68.7 reduce-scatter.36
  810.0 128.3 reduce-scatter.34
  941.9 128.2 reduce-scatter.32
  1073.7 161.2 reduce-scatter.46
  1238.4 161.2 reduce-scatter.42
  1403.2 161.1 reduce-scatter.44
  1567.9 161.1 reduce-scatter.40
  1733.0 61.3 reduce-scatter.50
  1798.2 61.2 reduce-scatter.54
  1863.4 61.2 reduce-scatter.48
  1928.4 61.2 reduce-scatter.52
  1992.5 131.5 all-reduce.3
where the time goes:
time: 2170 us; the launch traced here: 2160 us
  waiting for transfers between devices  1730 us (80%)
  blocking collectives  183 us (8%)
  matrix products  104 us (5%)
  local copies, waits for them, and re-layouts  87.5 us (4%)
  other arithmetic  33 us (2%)
    reduce_scatter x2, waiting for transfers between devices, sum_grads(): lax.psum_scatter(local[3], ('shard', 'ctx'), scatter_dimension=0, tiled=T...  330 us
    reduce_scatter x2, waiting for transfers between devices, sum_grads(): lax.psum_scatter(local[2], ('shard', 'ctx'), scatter_dimension=0, tiled=T...  329 us
    reduce_scatter x2, waiting for transfers between devices, sum_grads(): lax.psum_scatter(local[0], ('shard', 'ctx'), scatter_dimension=0, tiled=T...  264 us
    unnamed x29, waiting for transfers between devices  254 us
    all_gather x2, waiting for transfers between devices, fetch_weights(): lax.all_gather(shards[3], ('shard', 'ctx'), axis=0, tiled=True)  151 us
    psum x1, waiting for transfers between devices, sum_grads(): lax.psum((owned[0], owned[1], owned[2], owned[3], owned[4], owned[5]), 'r...  120 us
    reduce_scatter x2, waiting for transfers between devices, sum_grads(): lax.psum_scatter(local[1], ('shard', 'ctx'), scatter_dimension=0, tiled=T...  97.7 us
    all_gather x2, blocking collectives, fetch_weights(): lax.all_gather(shards[5], ('shard', 'ctx'), axis=1, tiled=True)  76.3 us
  transfers between devices with their start and end apart: 25, of which 22 were waited for; matrix products, arithmetic and copies ran while one was open for 8% of the time, Pallas kernels for 0%

commit v1 on v0

--- a/solution.py
+++ b/solution.py
@@ -14,6 +14,19 @@
 RATE_VECTOR = 0.1
 DECAY = 0.01
 NEGATIVE = -1e30
+
+
+def ring_gather(array, axis, dim):
+    size, index, extent = (lax.axis_size(axis), lax.axis_index(axis), array.shape[dim])
+    upward = [(i, (i + 1) % size) for i in range(size)]
+    out = jnp.zeros((*array.shape[:dim], size * extent, *array.shape[dim + 1 :]), array.dtype)
+    held = array
+    for step in range(size):
+        owner = (index - step) % size
+        out = lax.dynamic_update_slice_in_dim(out, held, owner * extent, axis=dim)
+        if step < size - 1:
+            held = lax.ppermute(held, axis, upward)
+    return out
 
 
 def narrow_value(array):
@@ -104,7 +117,7 @@
         lax.all_gather(shards[0], ("shard", "ctx"), axis=0, tiled=True),
         lax.all_gather(shards[1], ("shard", "ctx"), axis=0, tiled=True),
         lax.all_gather(shards[2], ("shard", "ctx"), axis=0, tiled=True),
-        lax.all_gather(shards[3], ("shard", "ctx"), axis=0, tiled=True),
+        ring_gather(shards[3], ("shard", "ctx"), 0),
         lax.all_gather(shards[4], ("shard", "ctx"), axis=1, tiled=True),
         lax.all_gather(shards[5], ("shard", "ctx"), axis=1, tiled=True),
     )

time: 2170 us -> 2100 us (0.968)
  waiting for transfers between devices: 1730 us -> 1590 us
  blocking collectives: 183 us -> 225 us
    all_gather x2 -> x0, waiting for transfers between devices: 151 us -> none  [fetch_weights(): lax.all_gather(shards[3], ('shard', 'ctx'), axis=0, tiled=True)]
    ppermute x0 -> x14, waiting for transfers between devices: none -> 127 us  [ring_gather(): held = lax.ppermute(held, axis, upward)]
    all_gather x2, waiting for transfers between devices: 64 us -> 0.02 us  [fetch_weights(): lax.all_gather(shards[0], ('shard', 'ctx'), axis=0, tiled=True)]
    all_gather x2, waiting for transfers between devices: 38.8 us -> 0.02 us  [fetch_weights(): lax.all_gather(shards[1], ('shard', 'ctx'), axis=0, tiled=True)]
    unnamed x29 -> x27, waiting for transfers between devices: 254 us -> 252 us
  transfers between devices with their start and end apart: 25 -> 37, of which waited for: 22 -> 27; matrix products, arithmetic and copies ran while one was open for 8% -> 10% of each run, Pallas kernels for 0% -> 0%
where the time goes in v1:
time: 2100 us; the launch traced here: 2090 us
  waiting for transfers between devices  1590 us (76%)
  blocking collectives  225 us (11%)
  local copies, waits for them, and re-layouts  109 us (5%)
  matrix products  108 us (5%)
  other arithmetic  33.8 us (2%)
    reduce_scatter x2, waiting for transfers between devices, sum_grads(): lax.psum_scatter(local[2], ('shard', 'ctx'), scatter_dimension=0, tiled=T...  329 us
    reduce_scatter x2, waiting for transfers between devices, sum_grads(): lax.psum_scatter(local[3], ('shard', 'ctx'), scatter_dimension=0, tiled=T...  329 us
    reduce_scatter x2, waiting for transfers between devices, sum_grads(): lax.psum_scatter(local[0], ('shard', 'ctx'), scatter_dimension=0, tiled=T...  264 us
    unnamed x27, waiting for transfers between devices  252 us
    ppermute x14, waiting for transfers between devices, ring_gather(): held = lax.ppermute(held, axis, upward)  127 us
    psum x1, waiting for transfers between devices, sum_grads(): lax.psum((owned[0], owned[1], owned[2], owned[3], owned[4], owned[5]), 'r...  119 us
    reduce_scatter x2, waiting for transfers between devices, sum_grads(): lax.psum_scatter(local[1], ('shard', 'ctx'), scatter_dimension=0, tiled=T...  97.4 us
    all_gather x2, blocking collectives, fetch_weights(): lax.all_gather(shards[5], ('shard', 'ctx'), axis=1, tiled=True)  90.4 us
  transfers between devices with their start and end apart: 37, of which 27 were waited for; matrix products, arithmetic and copies ran while one was open for 10% of the time, Pallas kernels for 0%

profile of v1, /device:TPU:0, one launch (start us, length us, event | category | flops | bytes accessed | tf_op | source)
XLA Modules:
  0.0 2094.4 jit_solution(7861871159544097235)
XLA Ops:
  22.3 57.5 %all-gather.1 = bf16[1,11,768]{1,0,2:T(2,128)(2,1)S(1)} all-gather(bf16[1,11,96]{1,0,2:T(2,128)(2,1)S(1)} %get-tuple-element.203), channel_id=3, replica_groups=mesh['rep'=4,'shard'=4,'ctx'=2] {'shard','ctx'}, dimensions={2}, use_global_device_ids=true | all-gather | bytes 19008 | tf_op jit(solution)/shard_map/all_gather | solution.py:122
  80.4 32.3 %all-gather = bf16[1,2,768]{1,0,2:T(2,128)(2,1)S(1)} all-gather(bf16[1,2,96]{1,0,2:T(2,128)(2,1)S(1)} %get-tuple-element.201), channel_id=2, replica_groups=mesh['rep'=4,'shard'=4,'ctx'=2] {'shard','ctx'}, dimensions={2}, use_global_device_ids=true | all-gather | bytes 3456 | tf_op jit(solution)/shard_map/all_gather | solution.py:121
  113.2 32.9 %all-gather.6 = bf16[1,11,768]{1,0,2:T(2,128)(2,1)S(1)} all-gather(bf16[1,11,96]{1,0,2:T(2,128)(2,1)S(1)} %get-tuple-element.202), channel_id=8, replica_groups=mesh['rep'=4,'shard'=4,'ctx'=2] {'shard','ctx'}, dimensions={2}, use_global_device_ids=true | all-gather | bytes 19008 | tf_op jit(solution)/shard_map/all_gather | solution.py:122
  151.5 18.1 collective-permute-done.1
  170.2 10.9 slice_reduce_fusion.7
  187.2 18.4 collective-permute-done.2
  205.8 10.9 slice_reduce_fusion.1
  226.5 14.1 collective-permute-done.3
  246.6 50.1 %all-gather.5 = bf16[1,2,768]{1,0,2:T(2,128)(2,1)S(1)} all-gather(bf16[1,2,96]{1,0,2:T(2,128)(2,1)S(1)} %get-tuple-element.200), channel_id=7, replica_groups=mesh['rep'=4,'shard'=4,'ctx'=2] {'shard','ctx'}, dimensions={2}, use_global_device_ids=true | all-gather | bytes 3456 | tf_op jit(solution)/shard_map/all_gather | solution.py:121
  311.7 21.3 %collective-permute-done.11 = bf16[384,768]{1,0:T(8,128)(2,1)S(1)} collective-permute-done((bf16[384,768]{1,0:T(8,128)(2,1)}, bf16[384,768]{1,0:T(8,128)(2,1)S(1)}, u32[]{:S(2)}, u32[]{:S(2)}) %collective-permute-start.11) | collective-permute-done | bytes 589856 | tf_op jit(solution)/shard_map/ppermute | solution.py:28
  335.6 11.1 collective-permute-done.5
  353.3 18.7 collective-permute-done.12
  372.9 14.0 collective-permute-done.6
  390.5 14.8 all_gather.49
  433.7 11.3 all_gather.56
  465.1 41.6 %all-gather.27.cloned.1.call-done = bf16[1,768,3072]{2,1,0:T(8,128)(2,1)} async-done(((bf16[1,96,3072]{2,1,0:T(8,128)(2,1)}), bf16[1,768,3072]{2,1,0:T(8,128)(2,1)}) %all-gather.27.cloned.1.call-update) | async-done | bytes 4718608 | tf_op jit(solution)/shard_map/all_gather | solution.py:119
  529.9 15.8 reduce-scatter.27.cloned.1.call-done
  583.5 15.6 reduce-scatter.31.cloned.1.call-done
  648.3 24.6 %reduce-scatter.39.cloned.1.call-done = f32[96,768]{1,0:T(8,128)} async-done(((f32[768,768]{1,0:T(8,128)}), f32[96,768]{1,0:T(8,128)}) %reduce-scatter.39.cloned.1.call-update) | async-done | bytes 294928 | tf_op jit(solution)/shard_map/reduce_scatter | solution.py:129
  672.9 72.8 %reduce-scatter.37.cloned.1.call-done = f32[96,768]{1,0:T(8,128)} async-done(((f32[768,768]{1,0:T(8,128)}), f32[96,768]{1,0:T(8,128)}) %reduce-scatter.37.cloned.1.call-update) | async-done | bytes 294928 | tf_op jit(solution)/shard_map/reduce_scatter | solution.py:129
  745.8 132.1 %reduce-scatter.35.cloned.1.call-done = f32[96,2304]{1,0:T(8,128)} async-done(((f32[768,2304]{1,0:T(8,128)}), f32[96,2304]{1,0:T(8,128)}) %reduce-scatter.35.cloned.1.call-update) | async-done | bytes 884752 | tf_op jit(solution)/shard_map/reduce_scatter | solution.py:128
  877.8 131.9 %reduce-scatter.33.cloned.1.call-done = f32[96,2304]{1,0:T(8,128)} async-done(((f32[768,2304]{1,0:T(8,128)}), f32[96,2304]{1,0:T(8,128)}) %reduce-scatter.33.cloned.1.call-update) | async-done | bytes 884752 | tf_op jit(solution)/shard_map/reduce_scatter | solution.py:128
  1009.7 164.7 %reduce-scatter.43.cloned.1.call-done = f32[96,3072]{1,0:T(8,128)} async-done(((f32[768,3072]{1,0:T(8,128)}), f32[96,3072]{1,0:T(8,128)}) %reduce-scatter.43.cloned.1.call-update) | async-done | bytes 1179664 | tf_op jit(solution)/shard_map/reduce_scatter | solution.py:130
  1174.4 164.7 %reduce-scatter.47.cloned.1.call-done = f32[384,768]{1,0:T(8,128)} async-done(((f32[3072,768]{1,0:T(8,128)}), f32[384,768]{1,0:T(8,128)}) %reduce-scatter.47.cloned.1.call-update) | async-done | bytes 1179664 | tf_op jit(solution)/shard_map/reduce_scatter | solution.py:131
  1339.1 164.7 %reduce-scatter.41.cloned.1.call-done = f32[96,3072]{1,0:T(8,128)} async-done(((f32[768,3072]{1,0:T(8,128)}), f32[96,3072]{1,0:T(8,128)}) %reduce-scatter.41.cloned.1.call-update) | async-done | bytes 1179664 | tf_op jit(solution)/shard_map/reduce_scatter | solution.py:130
  1503.8 164.7 %reduce-scatter.45.cloned.1.call-done = f32[384,768]{1,0:T(8,128)} async-done(((f32[3072,768]{1,0:T(8,128)}), f32[384,768]{1,0:T(8,128)}) %reduce-scatter.45.cloned.1.call-update) | async-done | bytes 1179664 | tf_op jit(solution)/shard_map/reduce_scatter | solution.py:131
  1674.3 59.3 %reduce-scatter.51.cloned.1.call-done = f32[96,2]{1,0:T(8,128)} async-done(((f32[768,2]{1,0:T(8,128)}), f32[96,2]{1,0:T(8,128)}) %reduce-scatter.51.cloned.1.call-update) | async-done | bytes 784
  1734.4 64.1 %reduce-scatter.55.cloned.1.call-done = f32[96,11]{1,0:T(8,128)} async-done(((f32[768,11]{1,0:T(8,128)}), f32[96,11]{1,0:T(8,128)}) %reduce-scatter.55.cloned.1.call-update) | async-done | bytes 4240
  1800.5 63.1 %reduce-scatter.49.cloned.1.call-done = f32[96,2]{1,0:T(8,128)} async-done(((f32[768,2]{1,0:T(8,128)}), f32[96,2]{1,0:T(8,128)}) %reduce-scatter.49.cloned.1.call-update) | async-done | bytes 784
  1864.4 64.1 %reduce-scatter.53.cloned.1.call-done = f32[96,11]{1,0:T(8,128)} async-done(((f32[768,11]{1,0:T(8,128)}), f32[96,11]{1,0:T(8,128)}) %reduce-scatter.53.cloned.1.call-update) | async-done | bytes 4240
  1929.4 11.1 all-reduce
  1943.6 119.4 %all-reduce.4.cloned.1.call-done = (f32[1,96,2304]{2,1,0:T(8,128)}, f32[1,96,2304]{2,1,0:T(8,128)}, f32[1,96,768]{2,1,0:T(8,128)}, f32[1,96,768]{2,1,0:T(8,128)}...) async-done(((f32[1,96,2304]{2,1,0:T(8,128)}, f32[1,96,2304]{2,1,0:T(8,128)}, f32[1,96,768]{2,1,0:T(8,128)}, ...) | async-done | bytes 7077904 | tf_op jit(solution)/shard_map/psum | solution.py:135
  (554 shorter events, 267.2 us)
Async XLA Ops:
  7.2 325.7 %all-gather.25.cloned.1.call-start = ((), (), s32[]{:S(2)}) async-start(), calls=%async_computation.32 | async-start | bytes 1327104 | tf_op jit(solution)/shard_map/all_gather | solution.py:118
  9.1 378.7 %all-gather.17.cloned.1.call-start = ((), (), s32[]{:S(2)}) async-start(), calls=%async_computation.28 | async-start | bytes 3981312 | tf_op jit(solution)/shard_map/all_gather | solution.py:117
  11.7 406.4 %all-gather.19.cloned.1.call-start = ((), (), s32[]{:S(2)}) async-start(), calls=%async_computation.29 | async-start | bytes 1327104 | tf_op jit(solution)/shard_map/all_gather | solution.py:118
  12.5 407.4 %all-gather.21.cloned.1.call-start = ((), (), s32[]{:S(2)}) async-start(), calls=%async_computation.30 | async-start | bytes 5308416 | tf_op jit(solution)/shard_map/all_gather | solution.py:119
  14.0 412.8 %all-gather.23.cloned.1.call-start = ((), (), s32[]{:S(2)}) async-start(), calls=%async_computation.31 | async-start | bytes 3981312 | tf_op jit(solution)/shard_map/all_gather | solution.py:117
  14.6 492.1 %all-gather.27.cloned.1.call-start = ((), (), s32[]{:S(2)}) async-start(), calls=%async_computation.33 | async-start | bytes 5308416 | tf_op jit(solution)/shard_map/all_gather | solution.py:119
  17.5 129.5 %collective-permute-start = (bf16[384,768]{1,0:T(8,128)(2,1)}, bf16[384,768]{1,0:T(8,128)(2,1)}, u32[]{:S(2)}, u32[]{:S(2)}) collective-permute-start(bf16[384,768]{1,0:T(8,128)(2,1)} %get-tuple-element.174), channel_id=1, source_target_pairs={{0,1},{1,2},{2,3},{3,4},{4,5},{5,6},{6,7},{7,0},{8,9},{9,10},{10,1... | collective-permute-start | bytes 1769480 | tf_op jit(solution)/shard_map/ppermute | solution.py:28
  20.5 130.9 %collective-permute-start.7 = (bf16[384,768]{1,0:T(8,128)(2,1)}, bf16[384,768]{1,0:T(8,128)(2,1)}, u32[]{:S(2)}, u32[]{:S(2)}) collective-permute-start(bf16[384,768]{1,0:T(8,128)(2,1)} %get-tuple-element.173), channel_id=1, source_target_pairs={{0,1},{1,2},{2,3},{3,4},{4,5},{5,6},{6,7},{7,0},{8,9},{9,10},{10,1... | collective-permute-start | bytes 1769480 | tf_op jit(solution)/shard_map/ppermute | solution.py:28
  22.0 503.3 %reduce-scatter.25.cloned.1.call-start = ((), (), s32[]{:S(2)}) async-start(), calls=%async_computation.16 | async-start | bytes 1179648 | tf_op jit(solution)/shard_map/reduce_scatter | solution.py:259
  169.6 36.0 %collective-permute-start.2 = (bf16[384,768]{1,0:T(8,128)(2,1)S(1)}, bf16[384,768]{1,0:T(8,128)(2,1)S(1)}, u32[]{:S(2)}, u32[]{:S(2)}) collective-permute-start(bf16[384,768]{1,0:T(8,128)(2,1)S(1)} %collective-permute-done.1), channel_id=1, source_target_pairs={{0,1},{1,2},{2,3},{3,4},{4,5},{5,6},{6,7},{7,0},{8,9},{9,10},{10,1... | collective-permute-start | bytes 1769480 | tf_op jit(solution)/shard_map/ppermute | solution.py:28
  221.9 83.2 %collective-permute-start.10 = (bf16[384,768]{1,0:T(8,128)(2,1)}, bf16[384,768]{1,0:T(8,128)(2,1)}, u32[]{:S(2)}, u32[]{:S(2)}) collective-permute-start(bf16[384,768]{1,0:T(8,128)(2,1)} %collective-permute-done.9), channel_id=1, source_target_pairs={{0,1},{1,2},{2,3},{3,4},{4,5},{5,6},{6,7},{7,0},{8,9},{9,10},{10,1... | collective-permute-start | bytes 1769480 | tf_op jit(solution)/shard_map/ppermute | solution.py:28
  240.6 67.4 %collective-permute-start.4 = (bf16[384,768]{1,0:T(8,128)(2,1)}, bf16[384,768]{1,0:T(8,128)(2,1)}, u32[]{:S(2)}, u32[]{:S(2)}) collective-permute-start(bf16[384,768]{1,0:T(8,128)(2,1)} %collective-permute-done.3), channel_id=1, source_target_pairs={{0,1},{1,2},{2,3},{3,4},{4,5},{5,6},{6,7},{7,0},{8,9},{9,10},{10,1... | collective-permute-start | bytes 1769480 | tf_op jit(solution)/shard_map/ppermute | solution.py:28
  308.0 38.7 %collective-permute-start.5 = (bf16[384,768]{1,0:T(8,128)(2,1)}, bf16[384,768]{1,0:T(8,128)(2,1)S(1)}, u32[]{:S(2)}, u32[]{:S(2)}) collective-permute-start(bf16[384,768]{1,0:T(8,128)(2,1)} %collective-permute-done.4), channel_id=1, source_target_pairs={{0,1},{1,2},{2,3},{3,4},{4,5},{5,6},{6,7},{7,0},{8,9},{9,10},{10,1... | collective-permute-start | bytes 1769480 | tf_op jit(solution)/shard_map/ppermute | solution.py:28
  332.9 39.1 %collective-permute-start.12 = (bf16[384,768]{1,0:T(8,128)(2,1)S(1)}, bf16[384,768]{1,0:T(8,128)(2,1)}, u32[]{:S(2)}, u32[]{:S(2)}) collective-permute-start(bf16[384,768]{1,0:T(8,128)(2,1)S(1)} %collective-permute-done.11), channel_id=1, source_target_pairs={{0,1},{1,2},{2,3},{3,4},{4,5},{5,6},{6,7},{7,0},{8,9},{9,10},{10,1... | collective-permute-start | bytes 1769480 | tf_op jit(solution)/shard_map/ppermute | solution.py:28
  346.7 40.3 %collective-permute-start.6 = (bf16[384,768]{1,0:T(8,128)(2,1)S(1)}, bf16[384,768]{1,0:T(8,128)(2,1)S(1)}, u32[]{:S(2)}, u32[]{:S(2)}) collective-permute-start(bf16[384,768]{1,0:T(8,128)(2,1)S(1)} %collective-permute-done.5), channel_id=1, source_target_pairs={{0,1},{1,2},{2,3},{3,4},{4,5},{5,6},{6,7},{7,0},{8,9},{9,10},{10,1... | collective-permute-start | bytes 1769480 | tf_op jit(solution)/shard_map/ppermute | solution.py:28
  372.0 89.1 %collective-permute-start.13 = (bf16[384,768]{1,0:T(8,128)(2,1)}, bf16[384,768]{1,0:T(8,128)(2,1)}, u32[]{:S(2)}, u32[]{:S(2)}) collective-permute-start(bf16[384,768]{1,0:T(8,128)(2,1)} %collective-permute-done.12), channel_id=1, source_target_pairs={{0,1},{1,2},{2,3},{3,4},{4,5},{5,6},{6,7},{7,0},{8,9},{9,10},{10,1... | collective-permute-start | bytes 1769480 | tf_op jit(solution)/shard_map/ppermute | solution.py:28
  459.1 86.6 %reduce-scatter.27.cloned.1.call-start = ((), (), s32[]{:S(2)}) async-start(), calls=%async_computation.17 | async-start | bytes 1179648 | tf_op jit(solution)/shard_map/reduce_scatter | solution.py:260
  515.5 63.4 %reduce-scatter.29.cloned.1.call-start = ((), (), s32[]{:S(2)}) async-start(), calls=%async_computation.18 | async-start | bytes 1179648 | tf_op jit(solution)/shard_map/reduce_scatter | solution.py:259
  561.3 37.9 %reduce-scatter.31.cloned.1.call-start = ((), (), s32[]{:S(2)}) async-start(), calls=%async_computation.19 | async-start | bytes 1179648 | tf_op jit(solution)/shard_map/reduce_scatter | solution.py:260
  564.1 108.8 %reduce-scatter.39.cloned.1.call-start = ((), (), s32[]{:S(2)}) async-start(), calls=%async_computation.23 | async-start | bytes 2654208 | tf_op jit(solution)/shard_map/reduce_scatter | solution.py:129
  567.1 178.7 %reduce-scatter.37.cloned.1.call-start = ((), (), s32[]{:S(2)}) async-start(), calls=%async_computation.22 | async-start | bytes 2654208 | tf_op jit(solution)/shard_map/reduce_scatter | solution.py:129
  570.0 307.8 %reduce-scatter.35.cloned.1.call-start = ((), (), s32[]{:S(2)}) async-start(), calls=%async_computation.21 | async-start | bytes 7962624 | tf_op jit(solution)/shard_map/reduce_scatter | solution.py:128
  575.4 434.2 %reduce-scatter.33.cloned.1.call-start = ((), (), s32[]{:S(2)}) async-start(), calls=%async_computation.20 | async-start | bytes 7962624 | tf_op jit(solution)/shard_map/reduce_scatter | solution.py:128
  604.6 569.8 %reduce-scatter.43.cloned.1.call-start = ((), (), s32[]{:S(2)}) async-start(), calls=%async_computation.25 | async-start | bytes 10616832 | tf_op jit(solution)/shard_map/reduce_scatter | solution.py:130
  611.6 727.4 %reduce-scatter.47.cloned.1.call-start = ((), (), s32[]{:S(2)}) async-start(), calls=%async_computation.27 | async-start | bytes 10616832 | tf_op jit(solution)/shard_map/reduce_scatter | solution.py:131
  617.7 886.1 %reduce-scatter.41.cloned.1.call-start = ((), (), s32[]{:S(2)}) async-start(), calls=%async_computation.24 | async-start | bytes 10616832 | tf_op jit(solution)/shard_map/reduce_scatter | solution.py:130
  628.8 1039.6 %reduce-scatter.45.cloned.1.call-start = ((), (), s32[]{:S(2)}) async-start(), calls=%async_computation.26 | async-start | bytes 10616832 | tf_op jit(solution)/shard_map/reduce_scatter | solution.py:131
  635.0 1098.5 %reduce-scatter.51.cloned.1.call-start = ((), (), s32[]{:S(2)}) async-start(), calls=%async_computation.35 | async-start | bytes 442368
  636.7 1161.8 %reduce-scatter.55.cloned.1.call-start = ((), (), s32[]{:S(2)}) async-start(), calls=%async_computation.37 | async-start | bytes 442368
  638.4 1225.1 %reduce-scatter.49.cloned.1.call-start = ((), (), s32[]{:S(2)}) async-start(), calls=%async_computation.34 | async-start | bytes 442368
  646.7 1281.9 %reduce-scatter.53.cloned.1.call-start = ((), (), s32[]{:S(2)}) async-start(), calls=%async_computation.36 | async-start | bytes 442368
  648.3 1414.7 %all-reduce.4.cloned.1.call-start = ((), (), s32[]{:S(2)}) async-start(), calls=%async_computation.38 | async-start | bytes 14155776 | tf_op jit(solution)/shard_map/psum | solution.py:135
  (143 other events, 4609.0 us)
Sparse Core Ops, SparseCore 0:
  10.8 65.1 all-gather.24
  78.7 77.5 all-gather.16
  159.1 51.5 all-gather.18
  213.3 107.7 all-gather.20
  323.7 102.1 all-gather.22
  428.6 78.0 all-gather.26
  509.5 15.8 reduce-scatter.24
  528.2 17.4 reduce-scatter.26
  561.4 17.4 reduce-scatter.28
  581.6 17.4 reduce-scatter.30
  603.2 69.6 reduce-scatter.38
  676.9 68.8 reduce-scatter.36
  749.4 128.3 reduce-scatter.34
  881.3 128.2 reduce-scatter.32
  1013.1 161.2 reduce-scatter.42
  1177.8 161.1 reduce-scatter.46
  1342.5 161.2 reduce-scatter.40
  1507.2 161.1 reduce-scatter.44
  1672.3 61.2 reduce-scatter.50
  1737.2 61.1 reduce-scatter.54
  1802.3 61.1 reduce-scatter.48
  1867.4 61.1 reduce-scatter.52
  1931.4 131.5 all-reduce.3
